TPU v7x, 32 devices: a whole 2x2x4 slice. The times are simulated.
32 devices in a mesh: groups: 2 (over y), attn: 4 (over x, core), exp: 4 (over z).
Axes of the slice: x: 2, y: 2, z: 4, core: 2. Of those that a mesh axis runs over, the one named last changes fastest.
Arguments:
- queries: bfloat16 [64, 32, 4096], P(('groups', 'exp'), None, 'attn'), parts along dimension 0, may hold values from -20 to 20
- new_keys: bfloat16 [64, 32, 512], P(('groups', 'exp'), None, 'attn'), parts along dimension 0, may hold values from -4 to 4
- new_values: bfloat16 [64, 32, 512], P(('groups', 'exp'), None, 'attn'), parts along dimension 0, may hold values from -4 to 4
- cache_keys: bfloat16 [64, 256, 512], P(('groups', 'exp'), None, 'attn'), parts along dimension 0, may hold values from -4 to 4
- cache_values: bfloat16 [64, 256, 512], P(('groups', 'exp'), None, 'attn'), parts along dimension 0, may hold values from -4 to 4
- cache_len: int32 [64], P(('groups', 'exp')), parts along dimension 0, may hold values from 2 to 256, as said below
- out_weight: bfloat16 [4096, 2048], P('attn', 'exp'), may hold values from -4 to 4
- residual: float32 [2048, 2048], P(('groups', 'exp', 'attn')), parts along dimension 0, may hold values from -6 to 6
- norm_gain: float32 [2048], replicated, may hold values from 0.1 to 1.9
- expert_ids: int32 [2048, 8], P(('groups', 'exp', 'attn')), parts along dimension 0, may hold values from 0 to 15, all different within a row; in each aligned block of 64 rows (0 to 63, 64 to 127, ...) at most 64 rows name the same one
- gate_nums: int32 [2048, 8], P(('groups', 'exp', 'attn')), parts along dimension 0, may hold values from 1 to 16
- w_gate_up: bfloat16 [16, 2048, 1536], P(('attn', 'exp')), may hold values from -0.125 to 0.125
- w_down: bfloat16 [16, 768, 2048], P(('attn', 'exp')), may hold values from -0.21875 to 0.21875
Outputs:
- mixed: float32 [2048, 2048], P(('groups', 'exp', 'attn')), parts along dimension 0
There are 2 independent parts, one for each index of `groups`. A program takes and returns all parts, laid end to end along the dimension named above; an argument that names none is the same for every part. Nothing has to cross between parts.
Inputs may be any that keep to these rules, and one draw needn't show every extreme that they name: `cache_len`: number of valid cache slots of each session; some session has all 256. `expert_ids`: within the 64 rows of one device, no expert is named by more than 64 rows, and this bound is reached; each row names 8 distinct experts.
All inputs are finite; a program needn't handle non-finite values.
Results may differ from a plain program's by a relative error of at most 0.0038.
Values may be sent and summed in bfloat16 or wider, within the bound.
A program may use at most 128 MiB of HBM per device.

v0:
```python
import jax
import jax.numpy as jnp
from jax import lax
from jax.sharding import PartitionSpec as P

HD = 128


def attend_session(packed):
    q_s, k_new, v_new, k_old, v_old, length = packed
    n_new = q_s.shape[0]
    n_old = k_old.shape[0]
    kv_count = k_old.shape[-1] // HD
    group_size = q_s.shape[-1] // (kv_count * HD)
    q_four = q_s.reshape(n_new, kv_count, group_size, HD)
    k_old3 = k_old.reshape(n_old, kv_count, HD)
    v_old3 = v_old.reshape(n_old, kv_count, HD)
    k_new3 = k_new.reshape(n_new, kv_count, HD)
    v_new3 = v_new.reshape(n_new, kv_count, HD)
    scale = 1.0 / HD**0.5
    s_old = jnp.einsum("ikgd,jkd->kgij", q_four, k_old3, preferred_element_type=jnp.float32) * scale
    s_new = jnp.einsum("ikgd,jkd->kgij", q_four, k_new3, preferred_element_type=jnp.float32) * scale
    valid_old = jnp.arange(n_old, dtype=jnp.int32) < length
    s_old = jnp.where(valid_old[None, None, None, :], s_old, jnp.float32(-1e30))
    causal = (
        jnp.arange(n_new, dtype=jnp.int32)[None, :] <= jnp.arange(n_new, dtype=jnp.int32)[:, None]
    )
    s_new = jnp.where(causal[None, None], s_new, jnp.float32(-1e30))
    top = jnp.maximum(jnp.max(s_old, -1, keepdims=True), jnp.max(s_new, -1, keepdims=True))
    e_old = jnp.exp(s_old - top)
    e_new = jnp.exp(s_new - top)
    total = jnp.sum(e_old, -1, keepdims=True) + jnp.sum(e_new, -1, keepdims=True)
    p_old = (e_old / total).astype(jnp.bfloat16)
    p_new = (e_new / total).astype(jnp.bfloat16)
    out = jnp.einsum("kgij,jkd->ikgd", p_old, v_old3, preferred_element_type=jnp.float32)
    out = out + jnp.einsum("kgij,jkd->ikgd", p_new, v_new3, preferred_element_type=jnp.float32)
    return out.reshape(n_new, kv_count * group_size * HD).astype(jnp.bfloat16)


def shards(
    queries,
    new_keys,
    new_values,
    cache_keys,
    cache_values,
    cache_len,
    out_weight,
    residual,
    norm_gain,
    expert_ids,
    gate_nums,
    w_gate_up,
    w_down,
):
    attended = lax.map(
        attend_session, (queries, new_keys, new_values, cache_keys, cache_values, cache_len)
    )
    local_rows = attended.reshape(attended.shape[0] * attended.shape[1], attended.shape[2])
    spread = jnp.dot(
        lax.all_gather(local_rows, "exp", axis=0, tiled=True),
        out_weight,
        preferred_element_type=jnp.float32,
    )
    partial_value = lax.all_to_all(spread, "exp", split_axis=0, concat_axis=1, tiled=True)
    projected = lax.psum_scatter(partial_value, "attn", scatter_dimension=0, tiled=True)
    middle = residual + projected
    meansq = jnp.mean(middle * middle, -1, keepdims=True)
    normed = (middle * lax.rsqrt(meansq + 1e-06) * norm_gain).astype(jnp.bfloat16)
    tok_rows = expert_ids.shape[0]
    top_count = expert_ids.shape[1]
    exp_dev = w_gate_up.shape[0]
    hidden_units = w_down.shape[1]
    n_experts = exp_dev * lax.axis_size("attn") * lax.axis_size("exp")
    capacity = max(2, 2 * tok_rows * top_count // n_experts)
    flat_ids = expert_ids.reshape(-1)
    onehot = (flat_ids[:, None] == jnp.arange(n_experts, dtype=jnp.int32)[None, :]).astype(
        jnp.int32
    )
    before = jnp.cumsum(onehot, axis=0) - onehot
    slot = jnp.sum(before * onehot, -1)
    target = (flat_ids * capacity + slot).reshape(tok_rows, top_count)
    places = jnp.arange(n_experts * capacity, dtype=jnp.int32)
    placing = jnp.sum((places[:, None, None] == target[None, :, :]).astype(jnp.int32), -1).astype(
        jnp.bfloat16
    )
    sent = jnp.dot(placing, normed, preferred_element_type=jnp.float32).astype(jnp.bfloat16)
    sent = sent.reshape(n_experts, capacity, normed.shape[1])
    block = lax.all_to_all(sent, ("attn", "exp"), split_axis=0, concat_axis=0, tiled=True)
    n_src = block.shape[0] // exp_dev
    rows_four = block.reshape(n_src, exp_dev, block.shape[1], block.shape[2])
    both = jnp.einsum("sjmd,jdf->sjmf", rows_four, w_gate_up, preferred_element_type=jnp.float32)
    hidden = (jax.nn.silu(both[..., :hidden_units]) * both[..., hidden_units:]).astype(jnp.bfloat16)
    result = jnp.einsum("sjmf,jfd->sjmd", hidden, w_down, preferred_element_type=jnp.float32)
    result = result.astype(jnp.bfloat16).reshape(block.shape)
    returned = lax.all_to_all(result, ("attn", "exp"), split_axis=0, concat_axis=0, tiled=True)
    picked = (
        returned[flat_ids, slot].reshape(tok_rows, top_count, normed.shape[1]).astype(jnp.float32)
    )
    numer = gate_nums.astype(jnp.float32)
    weights = numer / jnp.sum(numer, -1, keepdims=True)
    return middle + jnp.sum(picked * weights[:, :, None], 1)


def solution(mesh):
    in_specs = (
        P(("groups", "exp"), None, "attn"),
        P(("groups", "exp"), None, "attn"),
        P(("groups", "exp"), None, "attn"),
        P(("groups", "exp"), None, "attn"),
        P(("groups", "exp"), None, "attn"),
        P(("groups", "exp")),
        P("attn", "exp"),
        P(("groups", "exp", "attn"), None),
        P(),
        P(("groups", "exp", "attn"), None),
        P(("groups", "exp", "attn"), None),
        P(("attn", "exp"), None, None),
        P(("attn", "exp"), None, None),
    )
    out_specs = P(("groups", "exp", "attn"), None)
    return jax.shard_map(shards, mesh=mesh, in_specs=in_specs, out_specs=out_specs, check_vma=False)
```

profile of v0, /device:TPU:11, one launch (start us, length us, event | category | flops | bytes accessed | tf_op | source)
XLA Modules:
  0.0 439.5 jit_solution(16870406145571783817)
XLA Ops:
  6.5 63.9 %while.10 = (s32[]{:T(128)}, bf16[8,32,1024]{2,1,0:T(8,128)(2,1)}, bf16[8,256,128]{2,1,0:T(8,128)(2,1)}, s32[8]{0:T(128)}, bf16[8,256,128]{2,1,0:T(8,128)(2,1)},...) while((s32[]{:T(128)}, bf16[8,32,1024]{2,1,0:T(8,128)(2,1)}, ...), condition=%wide.region_5.6_spmd, body=%wide.region_0.5_spmd.sunk | while | flops 38404864 | bytes 2165389 | solution.py:55
  6.5 1.5 dynamic_slice.54
  8.7 0.9 dynamic-slice_bitcast_fusion.2
  9.6 0.9 fusion.71
  10.5 1.1 fusion.72
  11.9 0.9 fusion.75
  12.8 1.1 fusion.76
  14.7 1.3 dynamic_slice.54
  16.7 0.9 dynamic-slice_bitcast_fusion.2
  17.6 0.9 fusion.71
  18.5 1.1 fusion.72
  19.9 0.9 fusion.75
  20.8 1.1 fusion.76
  22.6 1.3 dynamic_slice.54
  24.7 0.9 dynamic-slice_bitcast_fusion.2
  25.5 0.9 fusion.71
  26.5 1.1 fusion.72
  27.9 0.9 fusion.75
  28.8 1.1 fusion.76
  30.6 1.3 dynamic_slice.54
  33.5 0.9 fusion.71
  34.5 1.1 fusion.72
  35.8 0.9 fusion.75
  36.8 1.1 fusion.76
  38.6 1.3 dynamic_slice.54
  40.6 0.9 dynamic-slice_bitcast_fusion.2
  41.5 0.9 fusion.71
  42.4 1.1 fusion.72
  43.8 0.9 fusion.75
  44.7 1.1 fusion.76
  46.6 1.3 dynamic_slice.54
  48.6 0.9 dynamic-slice_bitcast_fusion.2
  49.5 0.9 fusion.71
  50.4 1.1 fusion.72
  51.8 0.9 fusion.75
  52.7 1.1 fusion.76
  54.5 1.3 dynamic_slice.54
  56.6 0.9 dynamic-slice_bitcast_fusion.2
  57.4 0.9 fusion.71
  58.4 1.1 fusion.72
  59.8 0.9 fusion.75
  60.7 1.1 fusion.76
  62.5 1.3 dynamic_slice.54
  64.5 0.9 dynamic-slice_bitcast_fusion.2
  65.4 0.9 fusion.71
  66.3 1.1 fusion.72
  67.7 0.9 fusion.75
  68.7 1.1 fusion.76
  70.6 45.3 %all-gather.2.cloned.1.call-done = bf16[1024,1024]{1,0:T(8,128)(2,1)} async-done(((bf16[256,1024]{1,0:T(8,128)(2,1)}), bf16[1024,1024]{1,0:T(8,128)(2,1)}) %all-gather.2.cloned.1.call-update) | async-done | bytes 2097168 | tf_op jit(solution)/shard_map/all_gather | solution.py:60
  115.9 3.1 fusion.53
  119.0 50.4 %all_to_all.29 = f32[4,256,512]{2,1,0:T(8,128)S(1)} all-to-all(f32[4,256,512]{2,1,0:T(8,128)S(1)} %bitcast.131), channel_id=1, replica_groups=mesh['groups'=2,'attn'=4,'exp'=4] {'exp'}, dimensions={0} | all-to-all | bytes 4194304 | tf_op jit(solution)/shard_map/all_to_all | solution.py:64
  169.4 1.6 copy.56
  171.3 1.2 reduce-window.6
  173.8 29.3 %reduce-scatter.2.cloned.1.call-done = f32[64,2048]{1,0:T(8,128)} async-done(((f32[256,2048]{1,0:T(8,128)}), f32[64,2048]{1,0:T(8,128)}) %reduce-scatter.2.cloned.1.call-update) | async-done | bytes 524304 | tf_op jit(solution)/shard_map/reduce_scatter | solution.py:65
  203.1 1.4 multiply_reduce_fusion
  205.2 1.3 convolution_convert_fusion.1
  206.6 97.7 %all_to_all.30 = bf16[16,64,2048]{2,1,0:T(8,128)(2,1)S(1)} all-to-all(bf16[16,64,2048]{2,1,0:T(8,128)(2,1)S(1)} %bitcast.126), channel_id=1, replica_groups=mesh['groups'=2,'attn'=4,'exp'=4] {'attn','exp'}, dimensions={0} | all-to-all | bytes 8388608 | tf_op jit(solution)/shard_map/all_to_all | solution.py:88
  304.3 6.6 %fusion.30 = f32[16,1,64,1536]{3,2,0,1:T(8,128)S(1)} fusion(bf16[16,64,2048]{2,1,0:T(8,128)(2,1)S(1)} %all_to_all.30, bf16[1,2048,1536]{2,1,0:T(8,128)(2,1)S(1)} %bitcast.135), kind=kOutput, calls=%fused_computation.42 | convolution fusion | flops 6442450944 | bytes 16777216 | tf_op jit(solution)/shard_map/sjmd,jdf->sjmf/dot_general | solution.py:91
  310.9 5.1 %convolution_convert_fusion = bf16[16,64,2048]{2,1,0:T(8,128)(2,1)} fusion(bf16[1,768,2048]{2,1,0:T(8,128)(2,1)S(1)} %copy-done, f32[16,1,64,1536]{3,2,0,1:T(8,128)S(1)} %fusion.30), kind=kOutput, calls=%fused_computation.45 | convolution fusion | flops 3228041216 | bytes 13631488 | tf_op jit(solution)/shard_map/sjmf,jfd->sjmd/dot_general | solution.py:93
  316.0 7.6 %all-to-all-start.2 = ((bf16[16,64,2048]{2,1,0:T(8,128)(2,1)}), bf16[16,64,2048]{2,1,0:T(8,128)(2,1)}, u32[]{:S(2)}, u32[]{:S(2)}) async-start(bf16[16,64,2048]{2,1,0:T(8,128)(2,1)} %convolution_convert_fusion), calls=%async_computation.3 | async-start | bytes 8388608 | tf_op jit(solution)/shard_map/all_to_all | solution.py:95
  323.9 90.5 %all-to-all-done.2 = bf16[16,64,2048]{2,1,0:T(8,128)(2,1)} async-done(((bf16[16,64,2048]{2,1,0:T(8,128)(2,1)}), bf16[16,64,2048]{2,1,0:T(8,128)(2,1)}, u32[]{:S(2)}, u32[]{:S(2)}) %all-to-all-start.2) | async-done | bytes 4194336 | tf_op jit(solution)/shard_map/all_to_all | solution.py:95
  414.3 13.0 %gather_fusion = bf16[512,2048]{1,0:T(8,128)(2,1)} fusion(bf16[16,64,2048]{2,1,0:T(8,128)(2,1)} %all-to-all-done.2, s32[512]{0:T(512)S(1)} %bitcast.125), kind=kCustom, calls=%fused_computation | custom fusion | bytes 4198400 | tf_op jit(solution)/shard_map/gather | solution.py:97
  427.3 3.4 fusion.33
  430.8 1.9 add.75
  (120 shorter events, 16.8 us)
Async XLA Ops:
  6.5 304.4 %copy-start = (bf16[1,768,2048]{2,1,0:T(8,128)(2,1)S(1)}, bf16[1,768,2048]{2,1,0:T(8,128)(2,1)}, u32[]{:S(2)}) copy-start(bf16[1,768,2048]{2,1,0:T(8,128)(2,1)} %param.27) | copy-start | bytes 9437188
  6.5 109.3 %all-gather.2.cloned.1.call-start = ((), (), s32[]{:S(2)}) async-start(), calls=%async_computation.4 | async-start | bytes 2621440 | tf_op jit(solution)/shard_map/all_gather | solution.py:60
  70.5 132.6 %reduce-scatter.2.cloned.1.call-start = ((), (), s32[]{:S(2)}) async-start(), calls=%async_computation.5 | async-start | bytes 2621440 | tf_op jit(solution)/shard_map/reduce_scatter | solution.py:65
  169.4 1.6 copy-start.2
  171.0 34.2 %copy-start.4 = (f32[2048]{0:T(1024)S(1)}, f32[2048]{0:T(1024)}, u32[]{:S(2)}) copy-start(f32[2048]{0:T(1024)} %param.23) | copy-start | bytes 24580
  204.4 0.8 copy-start.1
  205.2 99.1 %slice-start = ((s8[6291456]{0:T(1024)(128)(4,1)}), s8[4194304]{0:T(1024)(128)(4,1)S(1)}, s32[]{:S(2)}) async-start(s8[6291456]{0:T(1024)(128)(4,1)} %bitcast.134), calls=%async_computation.6 | async-start | bytes 8388608
  206.6 97.7 %slice-start.1 = ((s8[6291456]{0:T(1024)(128)(4,1)}), s8[2097152]{0:T(1024)(128)(4,1)S(1)}, s32[]{:S(2)}) async-start(s8[6291456]{0:T(1024)(128)(4,1)} %bitcast.134), calls=%async_computation.7 | async-start | bytes 4194304
  316.0 7.7 %copy-start.3 = (s32[64,8]{0,1:T(8,128)S(1)}, s32[64,8]{0,1:T(8,128)}, u32[]{:S(2)}) copy-start(s32[64,8]{0,1:T(8,128)} %param.25) | copy-start | bytes 6148
  316.0 98.3 %all-to-all-start.2 = ((bf16[16,64,2048]{2,1,0:T(8,128)(2,1)}), bf16[16,64,2048]{2,1,0:T(8,128)(2,1)}, u32[]{:S(2)}, u32[]{:S(2)}) async-start(bf16[16,64,2048]{2,1,0:T(8,128)(2,1)} %convolution_convert_fusion), calls=%async_computation.3 | async-start | bytes 8388608 | tf_op jit(solution)/shard_map/all_to_all | solution.py:95
Sparse Core Ops, SparseCore 0:
  70.6 45.1 all-gather.1
  171.1 31.8 reduce-scatter.1
where the time goes:
time: 447 us; the launch traced here: 440 us
  waiting for transfers between devices  165 us (37%)
  blocking collectives  148 us (33%)
  matrix products  48.7 us (11%)
  local copies, waits for them, and re-layouts  39.5 us (9%)
  other arithmetic  16.3 us (4%)
  between operations  13.5 us (3%)
  starting transfers between devices  7.65 us (2%)
    all_to_all x1, blocking collectives, shards(): lax.all_to_all(sent, ('attn', 'exp'), split_axis=0, concat_axis=0, tiled=...  97.7 us
    all_to_all x1, waiting for transfers between devices, shards(): lax.all_to_all(result, ('attn', 'exp'), split_axis=0, concat_axis=0, tile...  90.5 us
    all_to_all x1, blocking collectives, shards(): lax.all_to_all(spread, 'exp', split_axis=0, concat_axis=1, tiled=True)  50.4 us
    all_gather x1, waiting for transfers between devices, shards(): lax.all_gather(local_rows, 'exp', axis=0, tiled=True)  45.3 us
    reduce_scatter x1, waiting for transfers between devices, shards(): lax.psum_scatter(partial_value, 'attn', scatter_dimension=0, tiled=True)  29.3 us
    gather x1, local copies, waits for them, and re-layouts, shards(): returned[flat_ids, slot].reshape(tok_rows, top_count, normed.shape[1])  13 us
    dynamic_slice x8, local copies, waits for them, and re-layouts, shards(): lax.map(attend_session, (queries, new_keys, new_values, cache_keys, cache...  10.7 us
  transfers between devices with their start and end apart: 3, of which 3 were waited for; matrix products, arithmetic and copies ran while one was open for 1% of the time, Pallas kernels for 0%

commit v1 on v0

--- a/solution.py
+++ b/solution.py
@@ -1,9 +1,397 @@
 import jax
 import jax.numpy as jnp
 from jax import lax
+from jax.experimental import pallas as pl
+from jax.experimental.pallas import tpu as pltpu
 from jax.sharding import PartitionSpec as P
 
 HD = 128
+LANES = 128
+F32 = jnp.float32
+BF16 = jnp.bfloat16
+
+
+def places():
+    a = lax.axis_index("attn")
+    z = lax.axis_index("exp")
+    core = a + 1 - 2 * (a % 2)
+    across = (a + 2) % 4
+    planes = [z, z + 1 - 2 * (z % 2), (z + 2) % 4, 3 - z]
+    return a, z, core, across, planes
+
+
+def meet(a, z, core, across, planes):
+    barrier = pltpu.get_barrier_semaphore()
+    peers = [(core, z), (across, z)] + [(a, p) for p in planes[1:]]
+    for pa, pz in peers:
+        pl.semaphore_signal(
+            barrier,
+            inc=1,
+            device_id={"attn": pa, "exp": pz},
+            device_id_type=pl.DeviceIdType.MESH,
+        )
+    pl.semaphore_wait(barrier, len(peers))
+
+
+def copy_to(src, dst, sems, i, pa, pz):
+    return pltpu.make_async_remote_copy(
+        src_ref=src,
+        dst_ref=dst,
+        send_sem=sems[0].at[i],
+        recv_sem=sems[1].at[i],
+        device_id={"attn": pa, "exp": pz},
+        device_id_type=pl.DeviceIdType.MESH,
+    )
+
+
+def attend(q, k_new, v_new, k_old, v_old, length):
+    n_new, n_old = q.shape[0], k_old.shape[0]
+    kv_count = k_old.shape[1] // HD
+    group = q.shape[1] // (kv_count * HD)
+    scale = 1.0 / HD**0.5
+    dims = (((1,), (1,)), ((), ()))
+    heads = []
+    for j in range(kv_count):
+        cols = slice(j * HD, (j + 1) * HD)
+        rows = jnp.concatenate(
+            [q[:, (j * group + g) * HD : (j * group + g + 1) * HD] for g in range(group)], 0
+        )
+        s_old = lax.dot_general(rows, k_old[:, cols], dims, preferred_element_type=F32) * scale
+        s_new = lax.dot_general(rows, k_new[:, cols], dims, preferred_element_type=F32) * scale
+        valid = lax.broadcasted_iota(jnp.int32, s_old.shape, 1) < length
+        s_old = jnp.where(valid, s_old, F32(-1e30))
+        token = lax.broadcasted_iota(jnp.int32, (group, n_new, n_new), 1).reshape(s_new.shape)
+        causal = lax.broadcasted_iota(jnp.int32, s_new.shape, 1) <= token
+        s_new = jnp.where(causal, s_new, F32(-1e30))
+        top = jnp.maximum(jnp.max(s_old, -1, keepdims=True), jnp.max(s_new, -1, keepdims=True))
+        e_old = jnp.exp(s_old - top)
+        e_new = jnp.exp(s_new - top)
+        inv = 1.0 / (jnp.sum(e_old, -1, keepdims=True) + jnp.sum(e_new, -1, keepdims=True))
+        p_old = (e_old * inv).astype(BF16)
+        p_new = (e_new * inv).astype(BF16)
+        out = jnp.dot(p_old, v_old[:, cols], preferred_element_type=F32)
+        out = out + jnp.dot(p_new, v_new[:, cols], preferred_element_type=F32)
+        out = out.astype(BF16)
+        heads += [out[g * n_new : (g + 1) * n_new] for g in range(group)]
+    return jnp.concatenate(heads, 1)
+
+
+def project_kernel(
+    len_ref, q_ref, kn_ref, vn_ref, kc_ref, vc_ref, wo_ref, out_ref,
+    att, own, csend, crecv, xsend, xrecv, zsend, zrecv, gs, gr, ss, sr,
+):
+    a, z, core, across, planes = places()
+    opposite = (core + 2) % 4
+    meet(a, z, core, across, planes)
+    g, s = (gs, gr), (ss, sr)
+    n_chunk, rows = att.shape[1], att.shape[2]
+    n_new = q_ref.shape[1]
+    per = rows // n_new
+    width = wo_ref.shape[1]
+
+    def chunk_copy(k, j):
+        src = att.at[2, j] if k == 3 else att.at[0, j]
+        return copy_to(src, att.at[k, j], g, (k - 1) * n_chunk + j, a, planes[2 if k == 2 else 1])
+
+    @pl.loop(0, n_chunk)
+    def _(j):
+        for i in range(per):
+            t = j * per + i
+            att[0, j, i * n_new : (i + 1) * n_new, :] = attend(
+                q_ref[t], kn_ref[t], vn_ref[t], kc_ref[t], vc_ref[t], len_ref[t]
+            )
+        chunk_copy(2, j).start()
+        chunk_copy(1, j).start()
+
+    def product(k):
+        x = jnp.concatenate([att[k, a], att[k, across], att[k, core], att[k, opposite]], 0)
+        r = jnp.dot(x, wo_ref[...], preferred_element_type=F32)
+        own[k] = r[: 2 * rows]
+        csend[k] = r[2 * rows :]
+        core_copy(k).start()
+
+    def core_copy(k):
+        return copy_to(csend.at[k], crecv.at[k], s, k, core, z)
+
+    def x_copy(k):
+        return copy_to(xsend.at[k], xrecv.at[k], s, 4 + k, across, z)
+
+    def z_copy(k):
+        return copy_to(zsend.at[k - 1], zrecv.at[k - 1], s, 7 + k, a, planes[k])
+
+    def to_x(k):
+        core_copy(k).wait_recv()
+        xsend[k] = own[k, rows:, :] + crecv[k, rows:, :]
+        x_copy(k).start()
+
+    def to_z(k):
+        x_copy(k).wait_recv()
+        total = own[k, :rows, :] + crecv[k, :rows, :] + xrecv[k]
+        if k == 0:
+            out_ref[:, pl.ds(pl.multiple_of(z * width, LANES), width)] = total
+        else:
+            zsend[k - 1] = total
+            z_copy(k).start()
+
+    @pl.loop(0, n_chunk)
+    def _(j):
+        chunk_copy(2, j).wait_recv()
+        chunk_copy(3, j).start()
+
+    product(0)
+    for j in range(n_chunk):
+        chunk_copy(1, j).wait_recv()
+    product(1)
+    to_x(0)
+    product(2)
+    to_x(1)
+    to_z(0)
+    to_x(2)
+    to_z(1)
+    to_z(2)
+    for j in range(n_chunk):
+        chunk_copy(3, j).wait_recv()
+    product(3)
+    to_x(3)
+    to_z(3)
+    for k in range(1, 4):
+        z_copy(k).wait_recv()
+        out_ref[:, pl.ds(pl.multiple_of(planes[k] * width, LANES), width)] = zrecv[k - 1]
+
+    @pl.loop(0, n_chunk)
+    def _(j):
+        for k in range(1, 4):
+            chunk_copy(k, j).wait_send()
+
+    for k in range(4):
+        core_copy(k).wait_send()
+        x_copy(k).wait_send()
+        if k > 0:
+            z_copy(k).wait_send()
+
+
+def project(queries, new_keys, new_values, cache_keys, cache_values, cache_len, out_weight):
+    sessions, n_new, width = queries.shape
+    rows = sessions * n_new // 4
+    cols = out_weight.shape[1]
+    vmem = pl.BlockSpec(memory_space=pltpu.VMEM)
+    return pl.pallas_call(
+        project_kernel,
+        out_shape=jax.ShapeDtypeStruct((rows, 4 * cols), F32),
+        in_specs=[pl.BlockSpec(memory_space=pltpu.SMEM)] + [vmem] * 6,
+        out_specs=vmem,
+        scratch_shapes=[
+            pltpu.VMEM((4, 4, rows, width), BF16),
+            pltpu.VMEM((4, 2 * rows, cols), F32),
+            pltpu.VMEM((4, 2 * rows, cols), F32),
+            pltpu.VMEM((4, 2 * rows, cols), F32),
+            pltpu.VMEM((4, rows, cols), F32),
+            pltpu.VMEM((4, rows, cols), F32),
+            pltpu.VMEM((3, rows, cols), F32),
+            pltpu.VMEM((3, rows, cols), F32),
+            pltpu.SemaphoreType.DMA((12,)),
+            pltpu.SemaphoreType.DMA((12,)),
+            pltpu.SemaphoreType.DMA((11,)),
+            pltpu.SemaphoreType.DMA((11,)),
+        ],
+        compiler_params=pltpu.CompilerParams(
+            collective_id=0, has_side_effects=True, vmem_limit_bytes=40 << 20
+        ),
+    )(cache_len, queries, new_keys, new_values, cache_keys, cache_values, out_weight)
+
+
+def experts_kernel(
+    pay_ref, wgu_hbm, wd_hbm, out_ref,
+    wgu, wd, xall, hid, own, csend, crecv, xsend, xrecv, zsend, zrecv, wsem, gs, gr, ss, sr,
+):
+    a, z, core, across, planes = places()
+    load_gu = pltpu.make_async_copy(wgu_hbm.at[0], wgu, wsem.at[0])
+    load_d = pltpu.make_async_copy(wd_hbm.at[0], wd, wsem.at[1])
+    load_gu.start()
+    load_d.start()
+    meet(a, z, core, across, planes)
+    g, s = (gs, gr), (ss, sr)
+    rows, width = out_ref.shape
+    units = wd.shape[0]
+    mine = a * 4 + z
+
+    def z_in(k):
+        src = xall.at[2, 0] if k == 3 else xall.at[0, 0]
+        return copy_to(src, xall.at[k, 0], g, k - 1, a, planes[2 if k == 2 else 1])
+
+    def x_in(k):
+        return copy_to(xall.at[k, 0], xall.at[k, 1], g, 3 + k, across, z)
+
+    def core_in(k, i):
+        return copy_to(xall.at[k, i], xall.at[k, 2 + i], g, 7 + 2 * k + i, core, z)
+
+    def core_copy(k):
+        return copy_to(csend.at[k], crecv.at[k], s, k, core, z)
+
+    def x_copy(k):
+        return copy_to(xsend.at[k], xrecv.at[k], s, 4 + k, across, z)
+
+    def z_copy(k):
+        return copy_to(zsend.at[k - 1], zrecv.at[k - 1], s, 7 + k, a, planes[k])
+
+    def compute(k):
+        core_in(k, 0).wait_recv()
+        core_in(k, 1).wait_recv()
+        if k == 0:
+            load_gu.wait()
+        x = xall[k].reshape(4 * rows, width + LANES)[:, :width]
+        nums = xall[k].reshape(4 * rows, width + LANES)[:, width:].astype(F32)
+        lane = lax.broadcasted_iota(jnp.int32, nums.shape, 1)
+        num = jnp.sum(jnp.where(lane == mine, nums, F32(0)), -1, keepdims=True)
+        weight = num / jnp.sum(nums, -1, keepdims=True)
+
+        @pl.loop(0, units // 256)
+        def _(t):
+            at = pl.multiple_of(t * 256, 256)
+            gate = jnp.dot(x, wgu[:, pl.ds(at, 256)], preferred_element_type=F32)
+            up = jnp.dot(
+                x,
+                wgu[:, pl.ds(pl.multiple_of(units + t * 256, 256), 256)],
+                preferred_element_type=F32,
+            )
+            hid[:, pl.ds(at, 256)] = (gate / (1.0 + jnp.exp(-gate)) * up).astype(BF16)
+
+        if k == 0:
+            load_d.wait()
+
+        @pl.loop(0, width // 512)
+        def _(t):
+            at = pl.ds(pl.multiple_of(t * 512, 512), 512)
+            r = jnp.dot(hid[...], wd[:, at], preferred_element_type=F32) * weight
+            own[k, :, at] = r[: 2 * rows]
+            csend[k, :, at] = r[2 * rows :].astype(BF16)
+
+        core_copy(k).start()
+
+    def to_x(k):
+        core_copy(k).wait_recv()
+        xsend[k] = (own[k, rows:, :] + crecv[k, rows:, :].astype(F32)).astype(BF16)
+        x_copy(k).start()
+
+    def to_z(k):
+        x_copy(k).wait_recv()
+        total = own[k, :rows, :] + crecv[k, :rows, :].astype(F32) + xrecv[k].astype(F32)
+        if k == 0:
+            out_ref[...] = total
+        else:
+            zsend[k - 1] = total.astype(BF16)
+            z_copy(k).start()
+
+    xall[0, 0] = pay_ref[...]
+    z_in(2).start()
+    z_in(1).start()
+    x_in(0).start()
+    core_in(0, 0).start()
+
+    def pass_z(k):
+        z_in(k).wait_recv()
+        if k == 2:
+            z_in(3).start()
+        x_in(k).start()
+        core_in(k, 0).start()
+
+    def pass_x(k):
+        x_in(k).wait_recv()
+        core_in(k, 1).start()
+
+    pass_x(0)
+    pass_z(1)
+    pass_z(2)
+    compute(0)
+    pass_x(1)
+    pass_z(3)
+    to_x(0)
+    compute(1)
+    pass_x(2)
+    to_x(1)
+    to_z(0)
+    compute(2)
+    pass_x(3)
+    to_x(2)
+    to_z(1)
+    compute(3)
+    to_z(2)
+    to_x(3)
+    to_z(3)
+    for k in range(1, 4):
+        z_copy(k).wait_recv()
+    out_ref[...] += zrecv[0].astype(F32) + zrecv[1].astype(F32) + zrecv[2].astype(F32)
+    for k in range(4):
+        x_in(k).wait_send()
+        core_in(k, 0).wait_send()
+        core_in(k, 1).wait_send()
+        core_copy(k).wait_send()
+        x_copy(k).wait_send()
+        if k > 0:
+            z_in(k).wait_send()
+            z_copy(k).wait_send()
+
+
+def experts(payload, w_gate_up, w_down):
+    rows = payload.shape[0]
+    width = payload.shape[1] - LANES
+    units = w_down.shape[1]
+    vmem = pl.BlockSpec(memory_space=pltpu.VMEM)
+    hbm = pl.BlockSpec(memory_space=pl.ANY)
+    return pl.pallas_call(
+        experts_kernel,
+        out_shape=jax.ShapeDtypeStruct((rows, width), F32),
+        in_specs=[vmem, hbm, hbm],
+        out_specs=vmem,
+        scratch_shapes=[
+            pltpu.VMEM((width, 2 * units), BF16),
+            pltpu.VMEM((units, width), BF16),
+            pltpu.VMEM((4, 4, rows, width + LANES), BF16),
+            pltpu.VMEM((4 * rows, units), BF16),
+            pltpu.VMEM((4, 2 * rows, width), F32),
+            pltpu.VMEM((4, 2 * rows, width), BF16),
+            pltpu.VMEM((4, 2 * rows, width), BF16),
+            pltpu.VMEM((4, rows, width), BF16),
+            pltpu.VMEM((4, rows, width), BF16),
+            pltpu.VMEM((3, rows, width), BF16),
+            pltpu.VMEM((3, rows, width), BF16),
+            pltpu.SemaphoreType.DMA((2,)),
+            pltpu.SemaphoreType.DMA((15,)),
+            pltpu.SemaphoreType.DMA((15,)),
+            pltpu.SemaphoreType.DMA((11,)),
+            pltpu.SemaphoreType.DMA((11,)),
+        ],
+        compiler_params=pltpu.CompilerParams(
+            collective_id=1, has_side_effects=True, vmem_limit_bytes=48 << 20
+        ),
+    )(payload, w_gate_up, w_down)
+
+
+def grid_shards(
+    queries,
+    new_keys,
+    new_values,
+    cache_keys,
+    cache_values,
+    cache_len,
+    out_weight,
+    residual,
+    norm_gain,
+    expert_ids,
+    gate_nums,
+    w_gate_up,
+    w_down,
+):
+    projected = project(
+        queries, new_keys, new_values, cache_keys, cache_values, cache_len, out_weight
+    )
+    middle = residual + projected
+    meansq = jnp.mean(middle * middle, -1, keepdims=True)
+    normed = (middle * lax.rsqrt(meansq + 1e-06) * norm_gain).astype(BF16)
+    chosen = expert_ids[:, :, None] == jnp.arange(LANES, dtype=jnp.int32)[None, None, :]
+    nums = jnp.sum(jnp.where(chosen, gate_nums[:, :, None], 0), 1).astype(BF16)
+    payload = jnp.concatenate([normed, nums], 1)
+    return middle + experts(payload, w_gate_up, w_down)
 
 
 def attend_session(packed):
@@ -101,6 +489,10 @@
     return middle + jnp.sum(picked * weights[:, :, None], 1)
 
 
+def fits_grid(mesh):
+    return mesh.shape["attn"] == 4 and mesh.shape["exp"] == 4
+
+
 def solution(mesh):
     in_specs = (
         P(("groups", "exp"), None, "attn"),
@@ -118,4 +510,5 @@
         P(("attn", "exp"), None, None),
     )
     out_specs = P(("groups", "exp", "attn"), None)
-    return jax.shard_map(shards, mesh=mesh, in_specs=in_specs, out_specs=out_specs, check_vma=False)
+    body = grid_shards if fits_grid(mesh) else shards
+    return jax.shard_map(body, mesh=mesh, in_specs=in_specs, out_specs=out_specs, check_vma=False)

time: 447 us -> 140 us (0.31); the launches traced: 440 us -> 140 us
  waiting for transfers between devices: 165 us -> 0 us
  blocking collectives: 148 us -> 0 us
  Pallas kernels: 0 us -> 128 us
  matrix products: 48.7 us -> 0 us
  local copies, waits for them, and re-layouts: 39.5 us -> 8.41 us
  between operations: 13.5 us -> 0.08 us
  other arithmetic: 16.3 us -> 3.12 us
  starting transfers between devices: 7.65 us -> 0 us
    all_to_all x2 -> x0, blocking collectives: 148 us -> none  [the longest x1 97.7 us: shards(): lax.all_to_all(sent, ('attn', 'exp'), split_axis=0, concat_axis=0, tiled=...]
    pallas_call x0 -> x2, Pallas kernels: none -> 128 us  [the longest x1 74.1 us: experts(): pl.pallas_call(experts_kernel, out_shape=jax.ShapeDtypeStruct((rows, widt...]
    all_to_all x1 -> x0, waiting for transfers between devices: 90.5 us -> none  [shards(): lax.all_to_all(result, ('attn', 'exp'), split_axis=0, concat_axis=0, tile...]
    dot_general x36 -> x0, matrix products: 48.7 us -> none  [the longest x8 8.91 us: attend_session(): jnp.einsum('ikgd,jkd->kgij', q_four, k_old3, preferred_element_type=jnp.f...]
    all_gather x1 -> x0, waiting for transfers between devices: 45.3 us -> none  [shards(): lax.all_gather(local_rows, 'exp', axis=0, tiled=True)]
    reduce_scatter x1 -> x0, waiting for transfers between devices: 29.3 us -> none  [shards(): lax.psum_scatter(partial_value, 'attn', scatter_dimension=0, tiled=True)]
    gather x1 -> x0, local copies, waits for them, and re-layouts: 13 us -> none  [shards(): returned[flat_ids, slot].reshape(tok_rows, top_count, normed.shape[1])]
    dynamic_slice x8 -> x0, local copies, waits for them, and re-layouts: 10.7 us -> none  [shards(): lax.map(attend_session, (queries, new_keys, new_values, cache_keys, cache...]
  transfers between devices with their start and end apart: 3 -> 0, of which waited for: 3 -> 0; matrix products, arithmetic and copies ran while one was open for 1% -> 0% of each run, Pallas kernels for 0% -> 0%
where the time goes in v1:
time: 140 us
  Pallas kernels  128 us (91%)
  local copies, waits for them, and re-layouts  8.41 us (6%)
  other arithmetic  3.12 us (2%)
    pallas_call x1, Pallas kernels, experts(): pl.pallas_call(experts_kernel, out_shape=jax.ShapeDtypeStruct((rows, widt...  74.1 us
    pallas_call x1, Pallas kernels, project(): pl.pallas_call(project_kernel, out_shape=jax.ShapeDtypeStruct((rows, 4 *...  54 us
    unnamed x18, local copies, waits for them, and re-layouts  8.41 us

profile of v1, /device:TPU:11, one launch (start us, length us, event | category | flops | bytes accessed | tf_op | source)
XLA Modules:
  0.0 139.7 jit_solution(5181999636328628272)
XLA Ops:
  0.0 0.0 copy-start
  0.0 0.9 copy.16
  0.9 0.8 copy.17
  1.7 0.2 select_reduce_fusion
  2.0 0.0 copy-start.1
  2.0 1.2 copy-done.1
  3.2 0.0 copy-start.2
  3.2 1.0 copy-done.2
  4.2 0.0 copy-start.3
  4.2 1.0 copy-done.3
  5.3 0.0 copy-start.4
  5.3 1.0 copy-done.4
  6.3 0.0 copy-start.5
  6.3 0.8 copy-done.5
  7.2 0.0 copy-start.6
  7.2 0.8 copy-done.6
  8.0 0.0 copy-start.7
  8.0 0.7 copy-done.7
  8.7 54.0 %shard_map.127 = f32[64,2048]{1,0:T(8,128)S(1)} custom-call(s32[8]{0:T(128)S(1)} %copy-done.7, bf16[8,32,1024]{2,1,0:T(8,128)(2,1)S(1)} %copy-done.2, bf16[8,32,128]{2,1,0:T(8,128)(2,1)S(1)} %copy-done.5, bf16[8,32,128]{2,1,0:T(8,128)(2,1)S(1)} %copy-done.6, bf16[8,256,128]{2,1,0:T(8,128)(2,1)S(1)} %copy-done.3, bf16[8,256,128]{2,1,0:T(8,128)(2,1)S(1)} %copy-done.4, ...), custom_call_target="tpu_custom_call" | custom-call | tf_op jit(solution)/shard_map/pallas_call | solution.py:178
  62.6 1.2 multiply_reduce_fusion
  63.8 0.8 multiply_convert_fusion
  64.7 0.0 copy-done
  64.7 74.1 %shard_map.128 = f32[64,2048]{1,0:T(8,128)S(1)} custom-call(bf16[64,2176]{1,0:T(8,128)(2,1)S(1)} %pad_maximum_fusion.pay_ref, bf16[1,2048,1536]{2,1,0:T(8,128)(2,1)} %wgu_hbm.1, bf16[1,768,2048]{2,1,0:T(8,128)(2,1)S(1)} %copy-done), custom_call_target="tpu_custom_call" | custom-call | tf_op jit(solution)/shard_map/pallas_call | solution.py:341
  138.8 0.9 add.20
  (3 shorter events, 0.0 us)
Async XLA Ops:
  0.0 64.7 %copy-start = (bf16[1,768,2048]{2,1,0:T(8,128)(2,1)S(1)}, bf16[1,768,2048]{2,1,0:T(8,128)(2,1)}, u32[]{:S(2)}) copy-start(bf16[1,768,2048]{2,1,0:T(8,128)(2,1)} %wd_hbm.1) | copy-start | bytes 9437188
  2.0 1.2 copy-start.1
  3.2 1.0 copy-start.2
  4.2 1.0 copy-start.3
  5.3 1.0 copy-start.4
  6.3 0.8 copy-start.5
  7.2 0.8 copy-start.6
  8.0 0.7 copy-start.7

commit v2 on v1

--- a/solution.py
+++ b/solution.py
@@ -77,12 +77,29 @@
 
 
 def project_kernel(
-    len_ref, q_ref, kn_ref, vn_ref, kc_ref, vc_ref, wo_ref, out_ref,
-    att, own, csend, crecv, xsend, xrecv, zsend, zrecv, gs, gr, ss, sr,
+    len_ref, q_hbm, kn_hbm, vn_hbm, kc_hbm, vc_hbm, wo_hbm, out_ref,
+    q_ref, kn_ref, vn_ref, kc_ref, vc_ref, wo_ref, lsem, att, own, csend, crecv, xsend, xrecv, zsend, zrecv, gs, gr, ss, sr,
 ):
     a, z, core, across, planes = places()
     opposite = (core + 2) % 4
+    loads = [
+        pltpu.make_async_copy(src, dst, lsem.at[i])
+        for i, (src, dst) in enumerate(
+            [
+                (q_hbm, q_ref),
+                (kn_hbm, kn_ref),
+                (vn_hbm, vn_ref),
+                (kc_hbm, kc_ref),
+                (vc_hbm, vc_ref),
+                (wo_hbm, wo_ref),
+            ]
+        )
+    ]
+    for load in loads:
+        load.start()
     meet(a, z, core, across, planes)
+    for load in loads:
+        load.wait()
     g, s = (gs, gr), (ss, sr)
     n_chunk, rows = att.shape[1], att.shape[2]
     n_new = q_ref.shape[1]
@@ -121,16 +138,16 @@
 
     def to_x(k):
         core_copy(k).wait_recv()
-        xsend[k] = own[k, rows:, :] + crecv[k, rows:, :]
+        xsend[k] = (own[k, rows:, :] + crecv[k, rows:, :]).astype(BF16)
         x_copy(k).start()
 
     def to_z(k):
         x_copy(k).wait_recv()
-        total = own[k, :rows, :] + crecv[k, :rows, :] + xrecv[k]
+        total = own[k, :rows, :] + crecv[k, :rows, :] + xrecv[k].astype(F32)
         if k == 0:
             out_ref[:, pl.ds(pl.multiple_of(z * width, LANES), width)] = total
         else:
-            zsend[k - 1] = total
+            zsend[k - 1] = total.astype(BF16)
             z_copy(k).start()
 
     @pl.loop(0, n_chunk)
@@ -156,7 +173,7 @@
     to_z(3)
     for k in range(1, 4):
         z_copy(k).wait_recv()
-        out_ref[:, pl.ds(pl.multiple_of(planes[k] * width, LANES), width)] = zrecv[k - 1]
+        out_ref[:, pl.ds(pl.multiple_of(planes[k] * width, LANES), width)] = zrecv[k - 1].astype(F32)
 
     @pl.loop(0, n_chunk)
     def _(j):
@@ -178,24 +195,31 @@
     return pl.pallas_call(
         project_kernel,
         out_shape=jax.ShapeDtypeStruct((rows, 4 * cols), F32),
-        in_specs=[pl.BlockSpec(memory_space=pltpu.SMEM)] + [vmem] * 6,
+        in_specs=[pl.BlockSpec(memory_space=pltpu.SMEM)] + [pl.BlockSpec(memory_space=pl.ANY)] * 6,
         out_specs=vmem,
         scratch_shapes=[
+            pltpu.VMEM(queries.shape, BF16),
+            pltpu.VMEM(new_keys.shape, BF16),
+            pltpu.VMEM(new_values.shape, BF16),
+            pltpu.VMEM(cache_keys.shape, BF16),
+            pltpu.VMEM(cache_values.shape, BF16),
+            pltpu.VMEM(out_weight.shape, BF16),
+            pltpu.SemaphoreType.DMA((6,)),
             pltpu.VMEM((4, 4, rows, width), BF16),
             pltpu.VMEM((4, 2 * rows, cols), F32),
             pltpu.VMEM((4, 2 * rows, cols), F32),
             pltpu.VMEM((4, 2 * rows, cols), F32),
-            pltpu.VMEM((4, rows, cols), F32),
-            pltpu.VMEM((4, rows, cols), F32),
-            pltpu.VMEM((3, rows, cols), F32),
-            pltpu.VMEM((3, rows, cols), F32),
+            pltpu.VMEM((4, rows, cols), BF16),
+            pltpu.VMEM((4, rows, cols), BF16),
+            pltpu.VMEM((3, rows, cols), BF16),
+            pltpu.VMEM((3, rows, cols), BF16),
             pltpu.SemaphoreType.DMA((12,)),
             pltpu.SemaphoreType.DMA((12,)),
             pltpu.SemaphoreType.DMA((11,)),
             pltpu.SemaphoreType.DMA((11,)),
         ],
         compiler_params=pltpu.CompilerParams(
-            collective_id=0, has_side_effects=True, vmem_limit_bytes=40 << 20
+            collective_id=0, has_side_effects=True, vmem_limit_bytes=56 << 20
         ),
     )(cache_len, queries, new_keys, new_values, cache_keys, cache_values, out_weight)
 
@@ -220,6 +244,8 @@
         return copy_to(src, xall.at[k, 0], g, k - 1, a, planes[2 if k == 2 else 1])
 
     def x_in(k):
+        if k == 1:
+            return copy_to(xall.at[0, 1], xall.at[1, 1], g, 4, a, planes[1])
         return copy_to(xall.at[k, 0], xall.at[k, 1], g, 3 + k, across, z)
 
     def core_in(k, i):
@@ -292,32 +318,35 @@
         z_in(k).wait_recv()
         if k == 2:
             z_in(3).start()
-        x_in(k).start()
+        if k != 1:
+            x_in(k).start()
         core_in(k, 0).start()
 
     def pass_x(k):
         x_in(k).wait_recv()
+        if k == 0:
+            x_in(1).start()
         core_in(k, 1).start()
 
     pass_x(0)
     pass_z(1)
     pass_z(2)
+    pass_x(1)
     compute(0)
-    pass_x(1)
     pass_z(3)
-    to_x(0)
     compute(1)
     pass_x(2)
     to_x(1)
-    to_z(0)
+    pass_x(3)
     compute(2)
-    pass_x(3)
     to_x(2)
     to_z(1)
     compute(3)
+    to_x(3)
+    to_x(0)
     to_z(2)
-    to_x(3)
     to_z(3)
+    to_z(0)
     for k in range(1, 4):
         z_copy(k).wait_recv()
     out_ref[...] += zrecv[0].astype(F32) + zrecv[1].astype(F32) + zrecv[2].astype(F32)

time: 140 us -> 129 us (0.921)
  local copies, waits for them, and re-layouts: 8.41 us -> 1.73 us
  Pallas kernels: 128 us -> 124 us
    unnamed x18 -> x4, local copies, waits for them, and re-layouts: 8.41 us -> 1.73 us
    pallas_call x1, Pallas kernels: 54 us -> 51.1 us  [project(): pl.pallas_call(project_kernel, out_shape=jax.ShapeDtypeStruct((rows, 4 *...]
where the time goes in v2:
time: 129 us
  Pallas kernels  124 us (96%)
  other arithmetic  3.27 us (3%)
  local copies, waits for them, and re-layouts  1.73 us (1%)
    pallas_call x1, Pallas kernels, experts(): pl.pallas_call(experts_kernel, out_shape=jax.ShapeDtypeStruct((rows, widt...  72.9 us
    pallas_call x1, Pallas kernels, project(): pl.pallas_call(project_kernel, out_shape=jax.ShapeDtypeStruct((rows, 4 *...  51.1 us

profile of v2, /device:TPU:11, one launch (start us, length us, event | category | flops | bytes accessed | tf_op | source)
XLA Modules:
  0.0 129.0 jit_solution(8406523578823253682)
XLA Ops:
  0.0 0.0 copy-start
  0.0 0.9 copy.16
  0.9 0.8 copy.17
  1.7 0.2 select_reduce_fusion
  2.0 51.1 %shard_map.127 = f32[64,2048]{1,0:T(8,128)} custom-call(s32[8]{0:T(128)} %len_ref.1, bf16[8,32,1024]{2,1,0:T(8,128)(2,1)} %q_hbm.1, bf16[8,32,128]{2,1,0:T(8,128)(2,1)} %kn_hbm.1, bf16[8,32,128]{2,1,0:T(8,128)(2,1)} %vn_hbm.1, bf16[8,256,128]{2,1,0:T(8,128)(2,1)} %kc_hbm.1, bf16[8,256,128]{2,1,0:T(8,128)(2,1)} %vc_hbm.1, bf16[1024,512]{1,0:T(8,128)(2,1)} %wo_hbm.1), custom_call_target="tpu_custom_call" | custom-call | tf_op jit(solution)/shard_map/pallas_call | solution.py:195
  53.0 1.4 %multiply_reduce_fusion = (f32[64]{0:T(128)S(1)}, f32[64,2048]{1,0:T(8,128)S(1)}) fusion(f32[64,2048]{1,0:T(8,128)} %param.20, f32[64,2048]{1,0:T(8,128)} %shard_map.127), kind=kLoop, calls=%fused_computation.1 | loop fusion | flops 393152 | bytes 1573120 | tf_op jit(solution)/shard_map/reduce_sum | solution.py:418
  54.4 0.8 multiply_convert_fusion
  55.3 0.0 copy-done
  55.3 72.9 %shard_map.128 = f32[64,2048]{1,0:T(8,128)S(1)} custom-call(bf16[64,2176]{1,0:T(8,128)(2,1)S(1)} %pad_maximum_fusion.pay_ref, bf16[1,2048,1536]{2,1,0:T(8,128)(2,1)} %wgu_hbm.1, bf16[1,768,2048]{2,1,0:T(8,128)(2,1)S(1)} %copy-done), custom_call_target="tpu_custom_call" | custom-call | tf_op jit(solution)/shard_map/pallas_call | solution.py:370
  128.2 0.9 add.20
  (3 shorter events, 0.0 us)
Async XLA Ops:
  0.0 55.3 %copy-start = (bf16[1,768,2048]{2,1,0:T(8,128)(2,1)S(1)}, bf16[1,768,2048]{2,1,0:T(8,128)(2,1)}, u32[]{:S(2)}) copy-start(bf16[1,768,2048]{2,1,0:T(8,128)(2,1)} %wd_hbm.1) | copy-start | bytes 9437188

commit v3 on v2

--- a/solution.py
+++ b/solution.py
@@ -76,8 +76,39 @@
     return jnp.concatenate(heads, 1)
 
 
-def project_kernel(
-    len_ref, q_hbm, kn_hbm, vn_hbm, kc_hbm, vc_hbm, wo_hbm, out_ref,
+def layer_kernel(
+    len_ref, q_hbm, kn_hbm, vn_hbm, kc_hbm, vc_hbm, wo_hbm, res_hbm, wgu_hbm, wd_hbm,
+    gain_ref, ids_ref, gates_ref, mixed_ref, *scratch,
+):
+    n_project = 19
+    a, z, core, across, planes = places()
+    wgu, wd, xall, middle, wsem = scratch[n_project : n_project + 5]
+    loads = [
+        pltpu.make_async_copy(wgu_hbm.at[0], wgu, wsem.at[0]),
+        pltpu.make_async_copy(wd_hbm.at[0], wd, wsem.at[1]),
+        pltpu.make_async_copy(res_hbm, middle, wsem.at[2]),
+    ]
+    project_part(
+        len_ref, q_hbm, kn_hbm, vn_hbm, kc_hbm, vc_hbm, wo_hbm, mixed_ref, loads,
+        *scratch[:n_project],
+    )
+    loads[2].wait()
+    width = mixed_ref.shape[1]
+    middle[...] += mixed_ref[...]
+    m = middle[...]
+    meansq = jnp.mean(m * m, -1, keepdims=True)
+    xall[0, 0, :, :width] = (m * lax.rsqrt(meansq + 1e-06) * gain_ref[...]).astype(BF16)
+    expert = lax.broadcasted_iota(jnp.int32, (LANES, m.shape[0]), 0)
+    nums = jnp.zeros((LANES, m.shape[0]), F32)
+    for k in range(ids_ref.shape[0]):
+        num = gates_ref[k : k + 1, :].astype(F32)
+        nums = nums + jnp.where(expert == ids_ref[k : k + 1, :], num, F32(0))
+    xall[0, 0, :, width:] = nums.T.astype(BF16)
+    experts_part(mixed_ref, loads, *scratch[n_project:])
+
+
+def project_part(
+    len_ref, q_hbm, kn_hbm, vn_hbm, kc_hbm, vc_hbm, wo_hbm, out_ref, later,
     q_ref, kn_ref, vn_ref, kc_ref, vc_ref, wo_ref, lsem, att, own, csend, crecv, xsend, xrecv, zsend, zrecv, gs, gr, ss, sr,
 ):
     a, z, core, across, planes = places()
@@ -95,7 +126,7 @@
             ]
         )
     ]
-    for load in loads:
+    for load in loads + later:
         load.start()
     meet(a, z, core, across, planes)
     for load in loads:
@@ -187,82 +218,51 @@
             z_copy(k).wait_send()
 
 
-def project(queries, new_keys, new_values, cache_keys, cache_values, cache_len, out_weight):
-    sessions, n_new, width = queries.shape
-    rows = sessions * n_new // 4
-    cols = out_weight.shape[1]
-    vmem = pl.BlockSpec(memory_space=pltpu.VMEM)
-    return pl.pallas_call(
-        project_kernel,
-        out_shape=jax.ShapeDtypeStruct((rows, 4 * cols), F32),
-        in_specs=[pl.BlockSpec(memory_space=pltpu.SMEM)] + [pl.BlockSpec(memory_space=pl.ANY)] * 6,
-        out_specs=vmem,
-        scratch_shapes=[
-            pltpu.VMEM(queries.shape, BF16),
-            pltpu.VMEM(new_keys.shape, BF16),
-            pltpu.VMEM(new_values.shape, BF16),
-            pltpu.VMEM(cache_keys.shape, BF16),
-            pltpu.VMEM(cache_values.shape, BF16),
-            pltpu.VMEM(out_weight.shape, BF16),
-            pltpu.SemaphoreType.DMA((6,)),
-            pltpu.VMEM((4, 4, rows, width), BF16),
-            pltpu.VMEM((4, 2 * rows, cols), F32),
-            pltpu.VMEM((4, 2 * rows, cols), F32),
-            pltpu.VMEM((4, 2 * rows, cols), F32),
-            pltpu.VMEM((4, rows, cols), BF16),
-            pltpu.VMEM((4, rows, cols), BF16),
-            pltpu.VMEM((3, rows, cols), BF16),
-            pltpu.VMEM((3, rows, cols), BF16),
-            pltpu.SemaphoreType.DMA((12,)),
-            pltpu.SemaphoreType.DMA((12,)),
-            pltpu.SemaphoreType.DMA((11,)),
-            pltpu.SemaphoreType.DMA((11,)),
-        ],
-        compiler_params=pltpu.CompilerParams(
-            collective_id=0, has_side_effects=True, vmem_limit_bytes=56 << 20
-        ),
-    )(cache_len, queries, new_keys, new_values, cache_keys, cache_values, out_weight)
-
-
-def experts_kernel(
-    pay_ref, wgu_hbm, wd_hbm, out_ref,
-    wgu, wd, xall, hid, own, csend, crecv, xsend, xrecv, zsend, zrecv, wsem, gs, gr, ss, sr,
+def experts_part(
+    out_ref, loads,
+    wgu, wd, xall, middle, wsem, hid, own, csend, crecv, xsend, xrecv, zsend, zrecv, gs, gr, ss, sr,
 ):
     a, z, core, across, planes = places()
-    load_gu = pltpu.make_async_copy(wgu_hbm.at[0], wgu, wsem.at[0])
-    load_d = pltpu.make_async_copy(wd_hbm.at[0], wd, wsem.at[1])
-    load_gu.start()
-    load_d.start()
-    meet(a, z, core, across, planes)
+    load_gu, load_d = loads[:2]
     g, s = (gs, gr), (ss, sr)
     rows, width = out_ref.shape
     units = wd.shape[0]
     mine = a * 4 + z
 
-    def z_in(k):
-        src = xall.at[2, 0] if k == 3 else xall.at[0, 0]
-        return copy_to(src, xall.at[k, 0], g, k - 1, a, planes[2 if k == 2 else 1])
-
-    def x_in(k):
+    half = rows // 2
+
+    def part(ref, h):
+        return ref.at[pl.ds(h * half, half), :]
+
+    def rows_copy(ks, i, kd, j, index, h, pa, pz):
+        return copy_to(
+            part(xall.at[ks, i], h), part(xall.at[kd, j], h), g, 2 * index + h, pa, pz
+        )
+
+    def z_in(k, h):
+        return rows_copy(2 if k == 3 else 0, 0, k, 0, k - 1, h, a, planes[2 if k == 2 else 1])
+
+    def x_in(k, h):
         if k == 1:
-            return copy_to(xall.at[0, 1], xall.at[1, 1], g, 4, a, planes[1])
-        return copy_to(xall.at[k, 0], xall.at[k, 1], g, 3 + k, across, z)
-
-    def core_in(k, i):
-        return copy_to(xall.at[k, i], xall.at[k, 2 + i], g, 7 + 2 * k + i, core, z)
-
-    def core_copy(k):
-        return copy_to(csend.at[k], crecv.at[k], s, k, core, z)
-
-    def x_copy(k):
-        return copy_to(xsend.at[k], xrecv.at[k], s, 4 + k, across, z)
-
-    def z_copy(k):
-        return copy_to(zsend.at[k - 1], zrecv.at[k - 1], s, 7 + k, a, planes[k])
+            return rows_copy(0, 1, 1, 1, 4, h, a, planes[1])
+        return rows_copy(k, 0, k, 1, 3 + k, h, across, z)
+
+    def core_in(k, i, h):
+        return rows_copy(k, i, k, 2 + i, 7 + 2 * k + i, h, core, z)
+
+    def core_copy(k, h):
+        return copy_to(csend.at[k, h], crecv.at[k, h], s, 2 * k + h, core, z)
+
+    def x_copy(k, h):
+        return copy_to(xsend.at[k, h], xrecv.at[k, h], s, 2 * (4 + k) + h, across, z)
+
+    def z_copy(k, h):
+        return copy_to(zsend.at[k - 1, h], zrecv.at[k - 1, h], s, 2 * (7 + k) + h, a, planes[k])
 
     def compute(k):
-        core_in(k, 0).wait_recv()
-        core_in(k, 1).wait_recv()
+        for i in range(2):
+            for h in range(2):
+                core_in(k, i, h).wait_recv()
         if k == 0:
             load_gu.wait()
         x = xall[k].reshape(4 * rows, width + LANES)[:, :width]
@@ -285,55 +285,64 @@
         if k == 0:
             load_d.wait()
 
-        @pl.loop(0, width // 512)
-        def _(t):
-            at = pl.ds(pl.multiple_of(t * 512, 512), 512)
-            r = jnp.dot(hid[...], wd[:, at], preferred_element_type=F32) * weight
-            own[k, :, at] = r[: 2 * rows]
-            csend[k, :, at] = r[2 * rows :].astype(BF16)
-
-        core_copy(k).start()
+        for h in range(2):
+            for t in range(2):
+                lo = h * (width // 2) + t * (width // 4)
+                r = jnp.dot(hid[...], wd[:, lo : lo + width // 4], preferred_element_type=F32)
+                r = r * weight
+                at = slice(t * (width // 4), (t + 1) * (width // 4))
+                own[k, h, :, at] = r[: 2 * rows]
+                csend[k, h, :, at] = r[2 * rows :].astype(BF16)
+            core_copy(k, h).start()
 
     def to_x(k):
-        core_copy(k).wait_recv()
-        xsend[k] = (own[k, rows:, :] + crecv[k, rows:, :].astype(F32)).astype(BF16)
-        x_copy(k).start()
+        for h in range(2):
+            core_copy(k, h).wait_recv()
+            total = own[k, h, rows:, :] + crecv[k, h, rows:, :].astype(F32)
+            xsend[k, h] = total.astype(BF16)
+            x_copy(k, h).start()
 
     def to_z(k):
-        x_copy(k).wait_recv()
-        total = own[k, :rows, :] + crecv[k, :rows, :].astype(F32) + xrecv[k].astype(F32)
-        if k == 0:
-            out_ref[...] = total
-        else:
-            zsend[k - 1] = total.astype(BF16)
-            z_copy(k).start()
-
-    xall[0, 0] = pay_ref[...]
-    z_in(2).start()
-    z_in(1).start()
-    x_in(0).start()
-    core_in(0, 0).start()
+        for h in range(2):
+            x_copy(k, h).wait_recv()
+            total = own[k, h, :rows, :] + crecv[k, h, :rows, :].astype(F32)
+            total = total + xrecv[k, h].astype(F32)
+            if k == 0:
+                at = slice(h * (width // 2), (h + 1) * (width // 2))
+                out_ref[:, at] = middle[:, at] + total
+            else:
+                zsend[k - 1, h] = total.astype(BF16)
+                z_copy(k, h).start()
+
+    for h in range(2):
+        z_in(2, h).start()
+        x_in(0, h).start()
+        core_in(0, 0, h).start()
+    for h in range(2):
+        z_in(1, h).start()
 
     def pass_z(k):
-        z_in(k).wait_recv()
-        if k == 2:
-            z_in(3).start()
-        if k != 1:
-            x_in(k).start()
-        core_in(k, 0).start()
+        for h in range(2):
+            z_in(k, h).wait_recv()
+            if k == 2:
+                z_in(3, h).start()
+            if k != 1:
+                x_in(k, h).start()
+            core_in(k, 0, h).start()
 
     def pass_x(k):
-        x_in(k).wait_recv()
-        if k == 0:
-            x_in(1).start()
-        core_in(k, 1).start()
+        for h in range(2):
+            x_in(k, h).wait_recv()
+            if k == 0:
+                x_in(1, h).start()
+            core_in(k, 1, h).start()
 
     pass_x(0)
+    pass_z(2)
     pass_z(1)
-    pass_z(2)
-    pass_x(1)
     compute(0)
     pass_z(3)
+    pass_x(1)
     compute(1)
     pass_x(2)
     to_x(1)
@@ -347,53 +356,21 @@
     to_z(2)
     to_z(3)
     to_z(0)
-    for k in range(1, 4):
-        z_copy(k).wait_recv()
-    out_ref[...] += zrecv[0].astype(F32) + zrecv[1].astype(F32) + zrecv[2].astype(F32)
+    for h in range(2):
+        at = slice(h * (width // 2), (h + 1) * (width // 2))
+        for k in range(1, 4):
+            z_copy(k, h).wait_recv()
+            out_ref[:, at] += zrecv[k - 1, h].astype(F32)
     for k in range(4):
-        x_in(k).wait_send()
-        core_in(k, 0).wait_send()
-        core_in(k, 1).wait_send()
-        core_copy(k).wait_send()
-        x_copy(k).wait_send()
-        if k > 0:
-            z_in(k).wait_send()
-            z_copy(k).wait_send()
-
-
-def experts(payload, w_gate_up, w_down):
-    rows = payload.shape[0]
-    width = payload.shape[1] - LANES
-    units = w_down.shape[1]
-    vmem = pl.BlockSpec(memory_space=pltpu.VMEM)
-    hbm = pl.BlockSpec(memory_space=pl.ANY)
-    return pl.pallas_call(
-        experts_kernel,
-        out_shape=jax.ShapeDtypeStruct((rows, width), F32),
-        in_specs=[vmem, hbm, hbm],
-        out_specs=vmem,
-        scratch_shapes=[
-            pltpu.VMEM((width, 2 * units), BF16),
-            pltpu.VMEM((units, width), BF16),
-            pltpu.VMEM((4, 4, rows, width + LANES), BF16),
-            pltpu.VMEM((4 * rows, units), BF16),
-            pltpu.VMEM((4, 2 * rows, width), F32),
-            pltpu.VMEM((4, 2 * rows, width), BF16),
-            pltpu.VMEM((4, 2 * rows, width), BF16),
-            pltpu.VMEM((4, rows, width), BF16),
-            pltpu.VMEM((4, rows, width), BF16),
-            pltpu.VMEM((3, rows, width), BF16),
-            pltpu.VMEM((3, rows, width), BF16),
-            pltpu.SemaphoreType.DMA((2,)),
-            pltpu.SemaphoreType.DMA((15,)),
-            pltpu.SemaphoreType.DMA((15,)),
-            pltpu.SemaphoreType.DMA((11,)),
-            pltpu.SemaphoreType.DMA((11,)),
-        ],
-        compiler_params=pltpu.CompilerParams(
-            collective_id=1, has_side_effects=True, vmem_limit_bytes=48 << 20
-        ),
-    )(payload, w_gate_up, w_down)
+        for h in range(2):
+            x_in(k, h).wait_send()
+            core_in(k, 0, h).wait_send()
+            core_in(k, 1, h).wait_send()
+            core_copy(k, h).wait_send()
+            x_copy(k, h).wait_send()
+            if k > 0:
+                z_in(k, h).wait_send()
+                z_copy(k, h).wait_send()
 
 
 def grid_shards(
@@ -411,16 +388,62 @@
     w_gate_up,
     w_down,
 ):
-    projected = project(
-        queries, new_keys, new_values, cache_keys, cache_values, cache_len, out_weight
-    )
-    middle = residual + projected
-    meansq = jnp.mean(middle * middle, -1, keepdims=True)
-    normed = (middle * lax.rsqrt(meansq + 1e-06) * norm_gain).astype(BF16)
-    chosen = expert_ids[:, :, None] == jnp.arange(LANES, dtype=jnp.int32)[None, None, :]
-    nums = jnp.sum(jnp.where(chosen, gate_nums[:, :, None], 0), 1).astype(BF16)
-    payload = jnp.concatenate([normed, nums], 1)
-    return middle + experts(payload, w_gate_up, w_down)
+    rows, width = residual.shape
+    units = w_down.shape[1]
+    cols = out_weight.shape[1]
+    heads = queries.shape[2]
+    vmem = pl.BlockSpec(memory_space=pltpu.VMEM)
+    hbm = pl.BlockSpec(memory_space=pl.ANY)
+    return pl.pallas_call(
+        layer_kernel,
+        out_shape=jax.ShapeDtypeStruct((rows, width), F32),
+        in_specs=[pl.BlockSpec(memory_space=pltpu.SMEM)] + [hbm] * 9 + [vmem] * 3,
+        out_specs=vmem,
+        scratch_shapes=[
+            pltpu.VMEM(queries.shape, BF16),
+            pltpu.VMEM(new_keys.shape, BF16),
+            pltpu.VMEM(new_values.shape, BF16),
+            pltpu.VMEM(cache_keys.shape, BF16),
+            pltpu.VMEM(cache_values.shape, BF16),
+            pltpu.VMEM(out_weight.shape, BF16),
+            pltpu.SemaphoreType.DMA((6,)),
+            pltpu.VMEM((4, 4, rows, heads), BF16),
+            pltpu.VMEM((4, 2 * rows, cols), F32),
+            pltpu.VMEM((4, 2 * rows, cols), F32),
+            pltpu.VMEM((4, 2 * rows, cols), F32),
+            pltpu.VMEM((4, rows, cols), BF16),
+            pltpu.VMEM((4, rows, cols), BF16),
+            pltpu.VMEM((3, rows, cols), BF16),
+            pltpu.VMEM((3, rows, cols), BF16),
+            pltpu.SemaphoreType.DMA((12,)),
+            pltpu.SemaphoreType.DMA((12,)),
+            pltpu.SemaphoreType.DMA((11,)),
+            pltpu.SemaphoreType.DMA((11,)),
+            pltpu.VMEM((width, 2 * units), BF16),
+            pltpu.VMEM((units, width), BF16),
+            pltpu.VMEM((4, 4, rows, width + LANES), BF16),
+            pltpu.VMEM((rows, width), F32),
+            pltpu.SemaphoreType.DMA((3,)),
+            pltpu.VMEM((4 * rows, units), BF16),
+            pltpu.VMEM((4, 2, 2 * rows, width // 2), F32),
+            pltpu.VMEM((4, 2, 2 * rows, width // 2), BF16),
+            pltpu.VMEM((4, 2, 2 * rows, width // 2), BF16),
+            pltpu.VMEM((4, 2, rows, width // 2), BF16),
+            pltpu.VMEM((4, 2, rows, width // 2), BF16),
+            pltpu.VMEM((3, 2, rows, width // 2), BF16),
+            pltpu.VMEM((3, 2, rows, width // 2), BF16),
+            pltpu.SemaphoreType.DMA((30,)),
+            pltpu.SemaphoreType.DMA((30,)),
+            pltpu.SemaphoreType.DMA((22,)),
+            pltpu.SemaphoreType.DMA((22,)),
+        ],
+        compiler_params=pltpu.CompilerParams(
+            collective_id=0, has_side_effects=True, vmem_limit_bytes=58 << 20
+        ),
+    )(
+        cache_len, queries, new_keys, new_values, cache_keys, cache_values, out_weight,
+        residual, w_gate_up, w_down, norm_gain.reshape(1, width), expert_ids.T, gate_nums.T,
+    )
 
 
 def attend_session(packed):

time: 129 us -> 124 us (0.961)
  other arithmetic: 3.27 us -> 0 us
  Pallas kernels: 124 us -> 122 us
    pallas_call x2 -> x1, Pallas kernels: 124 us -> 122 us  [grid_shards(): pl.pallas_call(layer_kernel, out_shape=jax.ShapeDtypeStruct((rows, width)...]
    reduce_sum x2 -> x0, other arithmetic: 1.57 us -> none  [the longest x1 1.36 us: grid_shards(): meansq = jnp.mean(middle * middle, -1, keepdims=True)]
where the time goes in v3:
time: 124 us
  Pallas kernels  122 us (98%)
  local copies, waits for them, and re-layouts  1.87 us (2%)
    pallas_call x1, Pallas kernels, grid_shards(): pl.pallas_call(layer_kernel, out_shape=jax.ShapeDtypeStruct((rows, width)...  122 us

profile of v3, /device:TPU:11, one launch (start us, length us, event | category | flops | bytes accessed | tf_op | source)
XLA Modules:
  0.0 124.1 jit_solution(17895506510373585430)
XLA Ops:
  0.0 122.2 %shard_map.127 = f32[64,2048]{1,0:T(8,128)} custom-call(s32[8]{0:T(128)} %len_ref.1, bf16[8,32,1024]{2,1,0:T(8,128)(2,1)} %q_hbm.1, bf16[8,32,128]{2,1,0:T(8,128)(2,1)} %kn_hbm.1, bf16[8,32,128]{2,1,0:T(8,128)(2,1)} %vn_hbm.1, bf16[8,256,128]{2,1,0:T(8,128)(2,1)} %kc_hbm.1, bf16[8,256,128]{2,1,0:T(8,128)(2,1)} %vc_hbm.1, bf16[1024,512]{1,0:T(8,128)(2,1)} %wo_hbm.1, ...), custom_call_target="tpu_custom_call" | custom-call | tf_op jit(solution)/shard_map/pallas_call | solution.py:397
  122.3 1.9 %copy.15 = f32[64,2048]{1,0:T(8,128)} copy(f32[64,2048]{1,0:T(8,128)} %shard_map.127) | data formatting | bytes 1048576

commit v4 on v3

--- a/solution.py
+++ b/solution.py
@@ -318,8 +318,7 @@
         z_in(2, h).start()
         x_in(0, h).start()
         core_in(0, 0, h).start()
-    for h in range(2):
-        z_in(1, h).start()
+    z_in(1, 0).start()
 
     def pass_z(k):
         for h in range(2):
@@ -333,28 +332,29 @@
     def pass_x(k):
         for h in range(2):
             x_in(k, h).wait_recv()
-            if k == 0:
-                x_in(1, h).start()
             core_in(k, 1, h).start()
 
     pass_x(0)
     pass_z(2)
+    z_in(1, 1).start()
+    for h in range(2):
+        x_in(1, h).start()
+    compute(0)
+    pass_x(2)
+    pass_z(3)
+    compute(2)
+    to_x(2)
+    pass_x(3)
     pass_z(1)
-    compute(0)
-    pass_z(3)
+    compute(3)
+    to_x(3)
+    to_z(2)
     pass_x(1)
     compute(1)
-    pass_x(2)
     to_x(1)
-    pass_x(3)
-    compute(2)
-    to_x(2)
+    to_x(0)
+    to_z(3)
     to_z(1)
-    compute(3)
-    to_x(3)
-    to_x(0)
-    to_z(2)
-    to_z(3)
     to_z(0)
     for h in range(2):
         at = slice(h * (width // 2), (h + 1) * (width // 2))

time: 124 us -> 115 us (0.927)
  the two profiles are of different devices: /device:TPU:11 before, /device:TPU:0 now
where the time goes in v4:
time: 115 us
  Pallas kernels  113 us (98%)
  local copies, waits for them, and re-layouts  1.87 us (2%)
    pallas_call x1, Pallas kernels, grid_shards(): pl.pallas_call(layer_kernel, out_shape=jax.ShapeDtypeStruct((rows, width)...  113 us

profile of v4, /device:TPU:0, one launch (start us, length us, event | category | flops | bytes accessed | tf_op | source)
XLA Modules:
  0.0 115.3 jit_solution(14295372532840701876)
XLA Ops:
  0.0 113.4 %shard_map.127 = f32[64,2048]{1,0:T(8,128)} custom-call(s32[8]{0:T(128)} %len_ref.1, bf16[8,32,1024]{2,1,0:T(8,128)(2,1)} %q_hbm.1, bf16[8,32,128]{2,1,0:T(8,128)(2,1)} %kn_hbm.1, bf16[8,32,128]{2,1,0:T(8,128)(2,1)} %vn_hbm.1, bf16[8,256,128]{2,1,0:T(8,128)(2,1)} %kc_hbm.1, bf16[8,256,128]{2,1,0:T(8,128)(2,1)} %vc_hbm.1, bf16[1024,512]{1,0:T(8,128)(2,1)} %wo_hbm.1, ...), custom_call_target="tpu_custom_call" | custom-call | tf_op jit(solution)/shard_map/pallas_call | solution.py:397
  113.4 1.9 %copy.15 = f32[64,2048]{1,0:T(8,128)} copy(f32[64,2048]{1,0:T(8,128)} %shard_map.127) | data formatting | bytes 1048576
